TPU v7x, 32 devices: a whole 2x2x4 slice. The times are simulated.
32 devices in a mesh: seq: 8 (over y, x, core), batch: 4 (over z).
Axes of the slice: x: 2, y: 2, z: 4, core: 2. Of those that a mesh axis runs over, the one named last changes fastest.
Arguments:
- queries: bfloat16 [16, 4096], P('batch', 'seq'), may hold values from -210 to 210
- key_cache: bfloat16 [16, 1024, 2048], P('batch', 'seq'), may hold values from -6 to 6
- value_cache: bfloat16 [16, 1024, 2048], P('batch', 'seq'), may hold values from -12 to 12
- new_key: bfloat16 [16, 2048], P('batch'), may hold values from -6 to 6
- new_value: bfloat16 [16, 2048], P('batch'), may hold values from -12 to 12
- page_table: int32 [16, 8], P('batch', 'seq'), may hold values from 0 to 3, as said below
- counts: int32 [16, 8], P('batch', 'seq'), may hold values from 1 to 128
- offsets: int32 [16], P('batch'), may hold values from 0 to 896
- w_out: bfloat16 [4096, 4608], P('seq', 'batch'), may hold values from -0.09375 to 0.09375
Outputs:
- projected: bfloat16 [16, 4608], P('seq', 'batch')
Inputs may be any that keep to these rules, and one draw needn't show every extreme that they name: `page_table`: for each group of 4 requests and each index along seq, the slots of that index's 1 pages of the group's requests are all different.
All inputs are finite; a program needn't handle non-finite values.
Results may differ from a plain program's by a relative error of at most 0.005.
Values may be sent and summed in bfloat16 or wider, within the bound.
A program may use at most 64 MiB of HBM per device.

v0:
```python
import jax
import jax.numpy as jnp
from jax import lax
from jax.sharding import PartitionSpec as P

HEADS = 32
KVH = 16
HD = 128
QSCALAR = 144
floor_score = -1e30


def joined(x, axis, combine):
    everything = jax.tree.map(lambda part: lax.all_gather(part, axis), x)
    initial = jax.tree.map(lambda part: part[0], everything)

    def turn(k, so_far):
        return combine(so_far, jax.tree.map(lambda part: part[k], everything))

    return lax.fori_loop(1, lax.axis_size(axis), turn, initial)


def on_device(
    queries, key_cache, value_cache, new_key, new_value, page_table, counts, offsets, w_out
):
    requests = queries.shape[0]
    groups = HEADS // KVH
    cycle_size = lax.axis_size("seq")
    cycle_place = lax.axis_index("seq")
    head_count = HEADS // cycle_size
    pages_here = page_table.shape[1]
    page_len = key_cache.shape[1]
    score_multiplier = QSCALAR ** (-0.5)

    def own_heads(array_in):
        return lax.dynamic_slice_in_dim(array_in, cycle_place * head_count, head_count, 1)

    all_queries = lax.all_gather(queries, "seq", axis=1, tiled=True)
    query_lattice = all_queries.reshape(requests, KVH, groups, HD)
    key_rows = jnp.take(key_cache, page_table, axis=0).reshape(
        requests, pages_here * page_len, KVH, HD
    )
    value_rows = jnp.take(value_cache, page_table, axis=0).reshape(
        requests, pages_here * page_len, KVH, HD
    )
    scores = (
        jnp.einsum("bkgd,btkd->bkgt", query_lattice, key_rows, preferred_element_type=jnp.float32)
        * score_multiplier
    )
    token_index = jnp.arange(page_len, dtype=jnp.int32)
    page_start = (cycle_place * pages_here + jnp.arange(pages_here, dtype=jnp.int32)) * page_len
    live_mask = (token_index[None, None, :] < counts[:, :, None]) & (
        page_start[None, :, None] + token_index[None, None, :] >= offsets[:, None, None]
    )
    live_mask = live_mask.reshape(requests, pages_here * page_len)[:, None, None, :]
    peak_score = jnp.max(jnp.where(live_mask, scores, floor_score), axis=-1)
    weights = jnp.where(live_mask, jnp.exp(scores - peak_score[..., None]), 0.0)
    block_total = jnp.sum(weights, axis=-1)
    block_sum = jnp.einsum(
        "bkgt,btkd->bkgd",
        weights.astype(jnp.bfloat16),
        value_rows,
        preferred_element_type=jnp.float32,
    )
    incoming_score = (
        jnp.einsum(
            "pcoz,pcz->pco",
            query_lattice,
            new_key.reshape(requests, KVH, HD),
            preferred_element_type=jnp.float32,
        )
        * score_multiplier
    )
    fresh_value = jnp.broadcast_to(
        new_value.astype(jnp.float32).reshape(requests, KVH, 1, HD), (requests, KVH, groups, HD)
    ).reshape(requests, HEADS, HD)
    flat_peak = peak_score.reshape(requests, HEADS)
    flat_total = block_total.reshape(requests, HEADS)
    flat_sum = block_sum.reshape(requests, HEADS, HD)
    flat_new = incoming_score.reshape(requests, HEADS)
    mine_new = own_heads(flat_new)
    mine_value = own_heads(fresh_value)

    def combine(earlier, later):
        top_score = jnp.maximum(earlier[0], later[0])
        left_weight = jnp.exp(earlier[0] - top_score)
        trailing_weight = jnp.exp(later[0] - top_score)
        return (
            top_score,
            earlier[1] * left_weight + later[1] * trailing_weight,
            earlier[2] * left_weight[..., None] + later[2] * trailing_weight[..., None],
        )

    merged_peak, merged_total, merged_sum = joined(
        (flat_peak, flat_total, flat_sum), "seq", combine
    )
    head_peak = own_heads(merged_peak)
    top_score = jnp.maximum(head_peak, mine_new)
    factor = jnp.exp(head_peak - top_score)
    own_weight = jnp.exp(mine_new - top_score)
    denominator = own_heads(merged_total) * factor + own_weight
    numerator = own_heads(merged_sum) * factor[..., None] + own_weight[..., None] * mine_value
    attention = (
        (numerator / denominator[..., None]).astype(jnp.bfloat16).reshape(requests, head_count * HD)
    )
    everyone = lax.all_gather(attention, "batch", axis=0, tiled=True)
    projected = lax.psum_scatter(
        jnp.dot(everyone, w_out, preferred_element_type=jnp.float32),
        "seq",
        scatter_dimension=0,
        tiled=True,
    )
    return projected.astype(jnp.bfloat16)


def solution(mesh):
    placed = (
        P("batch", "seq"),
        P("batch", "seq", None),
        P("batch", "seq", None),
        P("batch", None),
        P("batch", None),
        P("batch", "seq"),
        P("batch", "seq"),
        P("batch"),
        P("seq", "batch"),
    )
    return jax.shard_map(
        on_device, mesh=mesh, in_specs=placed, out_specs=P("seq", "batch"), check_vma=False
    )
```

profile of v0, /device:TPU:0, one launch (start us, length us, event | category | flops | bytes accessed | tf_op | source)
XLA Modules:
  0.0 98.0 jit_solution(6286090056575001631)
XLA Ops:
  0.0 0.8 fusion.15
  0.8 0.8 copy-done
  1.6 2.0 %gather_fusion = bf16[4,128,2048]{2,1,0:T(8,128)(2,1)} fusion(bf16[4,128,2048]{2,1,0:T(8,128)(2,1)S(1)} %copy-done, s32[1024]{0:T(1024)S(1)} %pad_clamp_fusion), kind=kCustom, calls=%fused_computation.clone | custom fusion | bytes 4194320 | tf_op jit(solution)/shard_map/jit(_take)/gather | solution.py:40
  3.6 3.6 %gather_fusion.1 = bf16[4,128,2048]{2,1,0:T(8,128)(2,1)} fusion(bf16[4,128,2048]{2,1,0:T(8,128)(2,1)} %param.15, s32[1024]{0:T(1024)S(1)} %pad_clamp_fusion), kind=kCustom, calls=%fused_computation.1.clone | custom fusion | bytes 4194320 | tf_op jit(solution)/shard_map/jit(_take)/gather | solution.py:43
  7.2 4.0 %bitcast_select_fusion = (bf16[4,1,128,2048]{3,2,0,1:T(8,128)(2,1)}, bf16[4,1,128,2048]{3,2,0,1:T(8,128)(2,1)S(1)}) fusion(bf16[4,128,2048]{2,1,0:T(8,128)(2,1)} %gather_fusion.1, pred[4]{0:T(512)(128)(4,1)S(1)} %and_bitcast_fusion, bf16[4,128,2048]{2,1,0:T(8,128)(2,1)} %gather_fusion), kind=kLoop, calls=%fused_computation.10 | loop fusion | flops 2097152 | bytes 8388612 | tf_op jit(solution)/shard_map/jit(_take)/select_n | solution.py:43
  11.2 2.0 %copy.35 = bf16[64,8,16,128]{3,2,1,0:T(8,128)(2,1)} copy(bf16[64,8,16,128]{3,1,2,0:T(8,128)(2,1)S(1)} %bitcast.71) | data formatting | bytes 4194304
  13.3 10.6 %all_gather.15 = bf16[4,4096]{1,0:T(4,128)(2,1)S(1)} all-gather(bf16[4,512]{1,0:T(4,128)(2,1)S(1)} %copy-done.4), channel_id=1, replica_groups=mesh['seq'=8,'batch'=4] {'seq'}, dimensions={1}, use_global_device_ids=true | all-gather | bytes 36864 | tf_op jit(solution)/shard_map/all_gather | solution.py:38
  23.9 3.0 %select_reduce_fusion = (f32[4,16,2]{2,1,0:T(8,128)S(1)}, f32[4,16,128,2]{2,3,1,0:T(2,128)S(1)}) fusion(pred[4,128]{1,0:T(4,128)(4,1)S(1)} %fusion.13, bf16[4,16,2,128]{3,2,1,0:T(2,128)(2,1)S(1)} %reshape.104, bf16[4,128,16,128]{3,2,1,0:T(8,128)(2,1)} %bitcast.72), kind=kOutput, calls=%fused_computation.21 | convolution fusion | flops 4243328 | bytes 2196480 | tf_op jit(solution)/shard_map/bkgd,btkd->bkgt/dot_general | solution.py:47
  26.9 0.6 copy.36
  27.6 0.7 fusion.3
  28.3 9.8 %all_gather.18 = f32[8,4,32,128]{3,2,1,0:T(8,128)S(1)} all-gather(f32[1,4,32,128]{3,2,1,0:T(8,128)S(1)} %bitcast.76), channel_id=1, replica_groups=mesh['seq'=8,'batch'=4] {'seq'}, dimensions={0}, use_global_device_ids=true | all-gather | bytes 589824 | tf_op jit(solution)/shard_map/all_gather | solution.py:14
  38.1 0.3 bitcast_reduce_fusion
  38.4 0.2 copy.25
  38.7 7.9 %all_gather.17 = f32[8,4,32]{2,1,0:T(4,128)S(1)} all-gather(f32[1,4,32]{2,1,0:T(4,128)S(1)} %copy.26), channel_id=1, replica_groups=mesh['seq'=8,'batch'=4] {'seq'}, dimensions={0}, use_global_device_ids=true | all-gather | bytes 4608 | tf_op jit(solution)/shard_map/all_gather | solution.py:14
  46.6 0.2 copy.23
  46.9 8.9 %all_gather.16 = f32[8,4,32]{2,1,0:T(4,128)S(1)} all-gather(f32[1,4,32]{2,1,0:T(4,128)S(1)} %copy.24), channel_id=1, replica_groups=mesh['seq'=8,'batch'=4] {'seq'}, dimensions={0}, use_global_device_ids=true | all-gather | bytes 4608 | tf_op jit(solution)/shard_map/all_gather | solution.py:14
  55.8 1.1 %while.19 = (s32[]{:T(128)}, f32[4,32]{1,0:T(4,128)S(1)}, f32[4,32]{1,0:T(4,128)S(1)}, f32[4,32,128]{2,1,0:T(8,128)S(1)}, f32[8,4,32]{2,1,0:T(4,128)S(1)}, /*ind...) while((s32[]{:T(128)}, f32[4,32]{1,0:T(4,128)S(1)}, ...), condition=%wide.region_3.5_spmd, body=%wide.region_2.4_spmd.sunk | while | flops 49925 | bytes 201879 | solution.py:20
  55.8 0.1 fusion.29
  56.0 0.1 fusion.29
  56.1 0.1 fusion.29
  56.3 0.1 fusion.29
  56.5 0.1 fusion.29
  56.6 0.1 fusion.29
  56.8 0.1 fusion.29
  57.1 0.2 fusion.19
  57.3 0.2 copy.34
  57.6 0.1 copy.29
  58.0 13.4 %all-gather = bf16[4,4,512]{2,1,0:T(4,128)(2,1)S(1)} all-gather(bf16[1,4,512]{2,1,0:T(4,128)(2,1)S(1)} %reshape.129), channel_id=1, replica_groups=mesh['seq'=8,'batch'=4] {'batch'}, dimensions={0}, use_global_device_ids=true | all-gather | bytes 20480 | tf_op jit(solution)/shard_map/all_gather | solution.py:106
  71.5 1.5 %fusion.20 = f32[16,1152]{1,0:T(8,128)S(1)} fusion(bf16[16,512]{1,0:T(8,128)(2,1)S(1)} %reshape.130, bf16[512,1152]{1,0:T(8,128)(2,1)} %param.21), kind=kOutput, calls=%fused_computation.44 | convolution fusion | flops 18874368 | bytes 1269760 | tf_op jit(solution)/shard_map/dot_general | solution.py:108
  73.0 23.1 %all-reduce = bf16[16,1152]{1,0:T(8,128)(2,1)S(1)} all-reduce(f32[16,1152]{1,0:T(8,128)S(1)} %fusion.20), channel_id=2, replica_groups=mesh['seq'=8,'batch'=4] {'seq'}, use_global_device_ids=true, to_apply=%region_4.6.clone | all-reduce | flops 18432 | bytes 110592
  96.1 0.6 dynamic-slice
  97.4 0.6 dynamic-slice_convert_fusion
  (47 shorter events, 1.1 us)
Async XLA Ops:
  0.0 1.6 %copy-start = (bf16[4,128,2048]{2,1,0:T(8,128)(2,1)S(1)}, bf16[4,128,2048]{2,1,0:T(8,128)(2,1)}, u32[]{:S(2)}) copy-start(bf16[4,128,2048]{2,1,0:T(8,128)(2,1)} %param.14) | copy-start | bytes 6291460
  3.6 3.6 %copy-start.7 = (s32[4,1]{0,1:T(1,128)S(1)}, s32[4,1]{0,1:T(1,128)}, u32[]{:S(2)}) copy-start(s32[4,1]{0,1:T(1,128)} %param.18) | copy-start | bytes 52
  11.2 2.0 %copy-start.5 = (s32[4,1]{0,1:T(1,128)S(1)}, s32[4,1]{0,1:T(1,128)}, u32[]{:S(2)}) copy-start(s32[4,1]{0,1:T(1,128)} %param.19) | copy-start | bytes 52
  11.2 2.0 %copy-start.6 = (s32[4]{0:T(128)S(1)}, s32[4]{0:T(128)}, u32[]{:S(2)}) copy-start(s32[4]{0:T(128)} %param.20) | copy-start | bytes 52
  11.2 2.1 %copy-start.4 = (bf16[4,512]{1,0:T(4,128)(2,1)S(1)}, bf16[4,512]{1,0:T(4,128)(2,1)}, u32[]{:S(2)}) copy-start(bf16[4,512]{1,0:T(4,128)(2,1)} %param.13) | copy-start | bytes 12292
  23.9 3.0 %copy-start.1 = (bf16[4,1,128,2048]{3,2,0,1:T(8,128)(2,1)S(1)}, bf16[4,1,128,2048]{3,2,0,1:T(8,128)(2,1)}, u32[]{:S(2)}) copy-start(bf16[4,1,128,2048]{3,2,0,1:T(8,128)(2,1)} %get-tuple-element.215) | copy-start | bytes 6291460
  27.5 29.5 %copy-start.2 = (bf16[4,2048]{1,0:T(4,128)(2,1)S(1)}, bf16[4,2048]{1,0:T(4,128)(2,1)}, u32[]{:S(2)}) copy-start(bf16[4,2048]{1,0:T(4,128)(2,1)} %param.16) | copy-start | bytes 49156
  27.6 30.3 %copy-start.3 = (bf16[4,2048]{1,0:T(4,128)(2,1)S(1)}, bf16[4,2048]{1,0:T(4,128)(2,1)}, u32[]{:S(2)}) copy-start(bf16[4,2048]{1,0:T(4,128)(2,1)} %param.17) | copy-start | bytes 49156
  38.1 58.0 %copy-start.8 = (u32[32]{0:T(128)S(1)}, u32[32]{0:T(128)}, u32[]{:S(2)}) copy-start(u32[32]{0:T(128)} %constant.74) | copy-start | bytes 388
where the time goes:
time: 98.3 us; the launch traced here: 98 us
  blocking collectives  73.8 us (75%)
  local copies, waits for them, and re-layouts  11.6 us (12%)
  other arithmetic  6.21 us (6%)
  matrix products  5.44 us (6%)
    all_gather x3, blocking collectives, joined(): everything = jax.tree.map(lambda part: lax.all_gather(part, axis), x)  26.6 us
    unnamed x1, blocking collectives  23.1 us
    all_gather x1, blocking collectives, on_device(): everyone = lax.all_gather(attention, 'batch', axis=0, tiled=True)  13.4 us
    all_gather x1, blocking collectives, on_device(): all_queries = lax.all_gather(queries, 'seq', axis=1, tiled=True)  10.6 us
    unnamed x24, local copies, waits for them, and re-layouts  4.04 us
    select_n x1, other arithmetic, on_device(): jnp.take(value_cache, page_table, axis=0)  3.96 us
    gather x1, local copies, waits for them, and re-layouts, on_device(): jnp.take(value_cache, page_table, axis=0)  3.58 us
    dot_general x1, matrix products, on_device(): jnp.einsum('bkgd,btkd->bkgt', query_lattice, key_rows, preferred_element_...  3.01 us

commit v1 on v0

--- a/solution.py
+++ b/solution.py
@@ -8,6 +8,12 @@
 HD = 128
 QSCALAR = 144
 floor_score = -1e30
+
+
+def gather_blocks(x, mesh_axis, d):
+    parts = lax.all_gather(x, mesh_axis, axis=0, tiled=False)
+    out = jnp.concatenate(parts, axis=d)
+    return out
 
 
 def joined(x, axis, combine):
@@ -35,7 +41,7 @@
     def own_heads(array_in):
         return lax.dynamic_slice_in_dim(array_in, cycle_place * head_count, head_count, 1)
 
-    all_queries = lax.all_gather(queries, "seq", axis=1, tiled=True)
+    all_queries = gather_blocks(queries, "seq", 1)
     query_lattice = all_queries.reshape(requests, KVH, groups, HD)
     key_rows = jnp.take(key_cache, page_table, axis=0).reshape(
         requests, pages_here * page_len, KVH, HD

time: 98.3 us -> 98.3 us (level)
  no operation moved by 1% of the time
where the time goes in v1:
time: 98.3 us; the launch traced here: 98 us
  blocking collectives  73.8 us (75%)
  local copies, waits for them, and re-layouts  11.6 us (12%)
  other arithmetic  6.21 us (6%)
  matrix products  5.44 us (6%)
    all_gather x3, blocking collectives, joined(): everything = jax.tree.map(lambda part: lax.all_gather(part, axis), x)  26.6 us
    unnamed x1, blocking collectives  23.1 us
    all_gather x1, blocking collectives, on_device(): everyone = lax.all_gather(attention, 'batch', axis=0, tiled=True)  13.4 us
    all_gather x1, blocking collectives, gather_blocks(): parts = lax.all_gather(x, mesh_axis, axis=0, tiled=False)  10.6 us
    unnamed x24, local copies, waits for them, and re-layouts  4.04 us
    select_n x1, other arithmetic, on_device(): jnp.take(value_cache, page_table, axis=0)  3.96 us
    gather x1, local copies, waits for them, and re-layouts, on_device(): jnp.take(value_cache, page_table, axis=0)  3.58 us
    dot_general x1, matrix products, on_device(): jnp.einsum('bkgd,btkd->bkgt', query_lattice, key_rows, preferred_element_...  3.01 us

profile of v1, /device:TPU:0, one launch (start us, length us, event | category | flops | bytes accessed | tf_op | source)
XLA Modules:
  0.0 98.0 jit_solution(1977995981467387669)
XLA Ops:
  0.0 0.8 fusion.15
  0.8 0.8 copy-done
  1.6 2.0 %gather_fusion = bf16[4,128,2048]{2,1,0:T(8,128)(2,1)} fusion(bf16[4,128,2048]{2,1,0:T(8,128)(2,1)S(1)} %copy-done, s32[1024]{0:T(1024)S(1)} %pad_clamp_fusion), kind=kCustom, calls=%fused_computation.clone | custom fusion | bytes 4194320 | tf_op jit(solution)/shard_map/jit(_take)/gather | solution.py:46
  3.6 3.6 %gather_fusion.1 = bf16[4,128,2048]{2,1,0:T(8,128)(2,1)} fusion(bf16[4,128,2048]{2,1,0:T(8,128)(2,1)} %param.15, s32[1024]{0:T(1024)S(1)} %pad_clamp_fusion), kind=kCustom, calls=%fused_computation.1.clone | custom fusion | bytes 4194320 | tf_op jit(solution)/shard_map/jit(_take)/gather | solution.py:49
  7.2 4.0 %bitcast_select_fusion = (bf16[4,1,128,2048]{3,2,0,1:T(8,128)(2,1)}, bf16[4,1,128,2048]{3,2,0,1:T(8,128)(2,1)S(1)}) fusion(bf16[4,128,2048]{2,1,0:T(8,128)(2,1)} %gather_fusion.1, pred[4]{0:T(512)(128)(4,1)S(1)} %and_bitcast_fusion, bf16[4,128,2048]{2,1,0:T(8,128)(2,1)} %gather_fusion), kind=kLoop, calls=%fused_computation.10 | loop fusion | flops 2097152 | bytes 8388612 | tf_op jit(solution)/shard_map/jit(_take)/select_n | solution.py:49
  11.2 2.0 %copy.37 = bf16[64,8,16,128]{3,2,1,0:T(8,128)(2,1)} copy(bf16[64,8,16,128]{3,1,2,0:T(8,128)(2,1)S(1)} %bitcast.73) | data formatting | bytes 4194304
  13.3 10.6 %all-gather.1 = bf16[8,4,512]{2,1,0:T(4,128)(2,1)S(1)} all-gather(bf16[1,4,512]{2,1,0:T(4,128)(2,1)S(1)} %bitcast.83), channel_id=2, replica_groups=mesh['seq'=8,'batch'=4] {'seq'}, dimensions={0}, use_global_device_ids=true | all-gather | bytes 36864 | tf_op jit(solution)/shard_map/all_gather | solution.py:14
  23.9 3.0 %select_reduce_fusion = (f32[4,16,2]{2,1,0:T(8,128)S(1)}, f32[4,16,128,2]{2,3,1,0:T(2,128)S(1)}) fusion(pred[4,128]{1,0:T(4,128)(4,1)S(1)} %fusion.13, bf16[4,16,2,128]{3,2,1,0:T(2,128)(2,1)S(1)} %reshape_reshape.3, bf16[4,128,16,128]{3,2,1,0:T(8,128)(2,1)} %bitcast.74), kind=kOutput, calls=%fused_computation.21 | convolution fusion | flops 4243328 | bytes 2196480 | tf_op jit(solution)/shard_map/bkgd,btkd->bkgt/dot_general | solution.py:53
  26.9 0.6 copy.38
  27.6 0.7 fusion.3
  28.3 9.8 %all_gather.22 = f32[8,4,32,128]{3,2,1,0:T(8,128)S(1)} all-gather(f32[1,4,32,128]{3,2,1,0:T(8,128)S(1)} %bitcast.79), channel_id=1, replica_groups=mesh['seq'=8,'batch'=4] {'seq'}, dimensions={0}, use_global_device_ids=true | all-gather | bytes 589824 | tf_op jit(solution)/shard_map/all_gather | solution.py:20
  38.1 0.3 bitcast_reduce_fusion
  38.4 0.2 copy.27
  38.6 7.9 %all_gather.21 = f32[8,4,32]{2,1,0:T(4,128)S(1)} all-gather(f32[1,4,32]{2,1,0:T(4,128)S(1)} %copy.28), channel_id=1, replica_groups=mesh['seq'=8,'batch'=4] {'seq'}, dimensions={0}, use_global_device_ids=true | all-gather | bytes 4608 | tf_op jit(solution)/shard_map/all_gather | solution.py:20
  46.6 0.2 copy.25
  46.9 8.9 %all_gather.20 = f32[8,4,32]{2,1,0:T(4,128)S(1)} all-gather(f32[1,4,32]{2,1,0:T(4,128)S(1)} %copy.26), channel_id=1, replica_groups=mesh['seq'=8,'batch'=4] {'seq'}, dimensions={0}, use_global_device_ids=true | all-gather | bytes 4608 | tf_op jit(solution)/shard_map/all_gather | solution.py:20
  55.8 1.1 %while.19 = (s32[]{:T(128)}, f32[4,32]{1,0:T(4,128)S(1)}, f32[4,32]{1,0:T(4,128)S(1)}, f32[4,32,128]{2,1,0:T(8,128)S(1)}, f32[8,4,32]{2,1,0:T(4,128)S(1)}, /*ind...) while((s32[]{:T(128)}, f32[4,32]{1,0:T(4,128)S(1)}, ...), condition=%wide.region_3.5_spmd, body=%wide.region_2.4_spmd.sunk | while | flops 49925 | bytes 201879 | solution.py:26
  55.8 0.1 fusion.29
  55.9 0.1 fusion.29
  56.1 0.1 fusion.29
  56.3 0.1 fusion.29
  56.4 0.1 fusion.29
  56.6 0.1 fusion.29
  56.8 0.1 fusion.29
  57.1 0.2 fusion.19
  57.3 0.2 copy.36
  57.6 0.1 copy.31
  58.0 13.4 %all-gather.2 = bf16[4,4,512]{2,1,0:T(4,128)(2,1)S(1)} all-gather(bf16[1,4,512]{2,1,0:T(4,128)(2,1)S(1)} %reshape.132), channel_id=1, replica_groups=mesh['seq'=8,'batch'=4] {'batch'}, dimensions={0}, use_global_device_ids=true | all-gather | bytes 20480 | tf_op jit(solution)/shard_map/all_gather | solution.py:112
  71.5 1.5 %fusion.20 = f32[16,1152]{1,0:T(8,128)S(1)} fusion(bf16[16,512]{1,0:T(8,128)(2,1)S(1)} %reshape.133, bf16[512,1152]{1,0:T(8,128)(2,1)} %param.21), kind=kOutput, calls=%fused_computation.44 | convolution fusion | flops 18874368 | bytes 1269760 | tf_op jit(solution)/shard_map/dot_general | solution.py:114
  73.0 23.1 %all-reduce = bf16[16,1152]{1,0:T(8,128)(2,1)S(1)} all-reduce(f32[16,1152]{1,0:T(8,128)S(1)} %fusion.20), channel_id=3, replica_groups=mesh['seq'=8,'batch'=4] {'seq'}, use_global_device_ids=true, to_apply=%region_4.6.clone | all-reduce | flops 18432 | bytes 110592
  96.1 0.6 dynamic-slice
  97.4 0.6 dynamic-slice_convert_fusion
  (48 shorter events, 1.1 us)
Async XLA Ops:
  0.0 1.6 %copy-start = (bf16[4,128,2048]{2,1,0:T(8,128)(2,1)S(1)}, bf16[4,128,2048]{2,1,0:T(8,128)(2,1)}, u32[]{:S(2)}) copy-start(bf16[4,128,2048]{2,1,0:T(8,128)(2,1)} %param.14) | copy-start | bytes 6291460
  3.6 3.6 %copy-start.7 = (s32[4,1]{0,1:T(1,128)S(1)}, s32[4,1]{0,1:T(1,128)}, u32[]{:S(2)}) copy-start(s32[4,1]{0,1:T(1,128)} %param.18) | copy-start | bytes 52
  11.2 2.0 %copy-start.5 = (s32[4,1]{0,1:T(1,128)S(1)}, s32[4,1]{0,1:T(1,128)}, u32[]{:S(2)}) copy-start(s32[4,1]{0,1:T(1,128)} %param.19) | copy-start | bytes 52
  11.2 2.0 %copy-start.6 = (s32[4]{0:T(128)S(1)}, s32[4]{0:T(128)}, u32[]{:S(2)}) copy-start(s32[4]{0:T(128)} %param.20) | copy-start | bytes 52
  11.2 2.1 %copy-start.4 = (bf16[4,512]{1,0:T(4,128)(2,1)S(1)}, bf16[4,512]{1,0:T(4,128)(2,1)}, u32[]{:S(2)}) copy-start(bf16[4,512]{1,0:T(4,128)(2,1)} %param.13) | copy-start | bytes 12292
  23.9 3.0 %copy-start.1 = (bf16[4,1,128,2048]{3,2,0,1:T(8,128)(2,1)S(1)}, bf16[4,1,128,2048]{3,2,0,1:T(8,128)(2,1)}, u32[]{:S(2)}) copy-start(bf16[4,1,128,2048]{3,2,0,1:T(8,128)(2,1)} %get-tuple-element.215) | copy-start | bytes 6291460
  27.5 29.5 %copy-start.2 = (bf16[4,2048]{1,0:T(4,128)(2,1)S(1)}, bf16[4,2048]{1,0:T(4,128)(2,1)}, u32[]{:S(2)}) copy-start(bf16[4,2048]{1,0:T(4,128)(2,1)} %param.16) | copy-start | bytes 49156
  27.5 30.3 %copy-start.3 = (bf16[4,2048]{1,0:T(4,128)(2,1)S(1)}, bf16[4,2048]{1,0:T(4,128)(2,1)}, u32[]{:S(2)}) copy-start(bf16[4,2048]{1,0:T(4,128)(2,1)} %param.17) | copy-start | bytes 49156
  38.1 58.0 %copy-start.8 = (u32[32]{0:T(128)S(1)}, u32[32]{0:T(128)}, u32[]{:S(2)}) copy-start(u32[32]{0:T(128)} %constant.74) | copy-start | bytes 388
